TPU v7x, 256 devices: a whole 4x4x8 slice. The times are simulated.
256 devices in a mesh: depth: 64 (over z, y_lo, x), tile: 4 (over y_hi, core).
Axes of the slice: x: 4, y: 4 (y_hi: 2, y_lo: 2; y = y_hi * 2 + y_lo), z: 8, core: 2. Of those that a mesh axis runs over, the one named last changes fastest.
Arguments:
- volume: float32 [2, 64, 225, 512], P(None, 'depth', None, 'tile'), may hold values from 0.1 to 5
- kernel: bfloat16 [64, 225, 81, 225], P('depth'), as said below
- measured: float32 [2, 225, 512], P(None, None, 'tile'), may hold values from 0.2 to 5
Outputs:
- updated: float32 [2, 64, 225, 512], P(None, 'depth', None, 'tile')
Inputs may be any that keep to these rules, and one draw needn't show every extreme that they name: `kernel`: kernel weights are nonnegative.
All inputs are finite; a program needn't handle non-finite values.
Results may differ from a plain program's by a relative error of at most 0.0015.
Values may be sent and summed in bfloat16 or wider, within the bound.
A program may use at most 128 MiB of HBM per device.

v0:
```python
import jax
import jax.numpy as jnp
from jax import lax
from jax.sharding import PartitionSpec as P

KSIDE = 9
COLS = 32


def with_halo(cells, sides, width):
    for axis, dim in sides:
        count = lax.axis_size(axis)
        ends = count - 1
        head = lax.slice_in_dim(cells, 0, width, axis=dim)
        tail = lax.slice_in_dim(cells, cells.shape[dim] - width, cells.shape[dim], axis=dim)
        cells = jnp.concatenate(
            [
                lax.ppermute(tail, axis, [(i, (i + 1) % count) for i in range(ends)]),
                cells,
                lax.ppermute(head, axis, [((i + 1) % count, i) for i in range(ends)]),
            ],
            axis=dim,
        )
    return cells


def stacked(flat, sign, axis, cols, cells):
    half = KSIDE // 2
    extended = jnp.pad(flat, ((0, 0), (half, half)))
    column = lax.iota(jnp.int32, cells) % cols
    pieces = []
    for shift_a in range(-half, half + 1):
        for shift_b in range(-half, half + 1):
            start = (half + sign * shift_a) * cols + half + sign * shift_b
            piece = extended[:, start : start + cells]
            moved = column + sign * shift_b
            keep = (moved >= 0) & (moved < cols)
            pieces.append(jnp.where(keep[None, :], piece, jnp.zeros_like(piece)))
    return jnp.stack(pieces, axis=axis)


def local(volume, kernel, measured):
    frames, local_depths, phases, cells = volume.shape
    cols = COLS
    half = KSIDE // 2
    offsets = kernel.shape[2]
    vol16 = volume.astype(jnp.bfloat16)
    rimmed = with_halo(vol16, (("tile", 3),), half * cols)
    partial_value = []
    for frame in range(frames):
        plane = 0
        flat = kernel[plane].reshape(phases, offsets * phases)
        spread = stacked(rimmed[frame, plane], 1, 0, cols, cells).reshape(offsets * phases, cells)
        total = jnp.dot(flat, spread, preferred_element_type=jnp.float32)
        partial_value.append(total)
    partial_value = jnp.stack(partial_value)
    projection = lax.psum(partial_value, "depth")
    ratio = (measured / projection).astype(jnp.bfloat16)
    ratio_rimmed = with_halo(ratio, (("tile", 2),), half * cols)
    spreads = [
        stacked(ratio_rimmed[frame], -1, 1, cols, cells).reshape(phases * offsets, cells)
        for frame in range(frames)
    ]
    plane = 0
    flat = kernel[plane].reshape(phases * offsets, phases)
    norm = jnp.sum(kernel[plane], axis=(0, 1), dtype=jnp.float32)
    backs = []
    for frame in range(frames):
        back = lax.dot_general(
            flat, spreads[frame], (((0,), (0,)), ((), ())), preferred_element_type=jnp.float32
        )
        backs.append(volume[frame, plane] * back / norm[:, None])
    planes = [jnp.stack(backs)]
    return jnp.stack(planes, axis=1)


def solution(mesh):
    in_specs = (P(None, "depth", None, "tile"), P("depth", None, None, None), P(None, None, "tile"))
    out_specs = P(None, "depth", None, "tile")
    return jax.shard_map(local, mesh=mesh, in_specs=in_specs, out_specs=out_specs, check_vma=False)
```

profile of v0, /device:TPU:1, one launch (start us, length us, event | category | flops | bytes accessed | tf_op | source)
XLA Modules:
  0.0 829.7 jit_solution(5707975148380617097)
XLA Ops:
  6.5 1.0 copy.22
  7.5 5.1 collective-permute-start.1
  12.6 3.0 collective-permute-start
  15.7 9.6 %copy.11 = bf16[1,225,81,225]{3,2,1,0:T(8,128)(2,1)} copy(bf16[1,225,81,225]{3,1,2,0:T(8,128)(2,1)} %param.4) | data formatting | bytes 16402500 | tf_op args[1]
  25.4 15.9 %reshape_squeeze.7 = bf16[225,18225]{1,0:T(8,128)(2,1)} reshape(bf16[1,225,81,225]{3,2,1,0:T(8,128)(2,1)} %copy.11) | data formatting | bytes 16402500 | tf_op jit(solution)/shard_map/reshape;squeeze | solution.py:52
  49.3 0.7 constant_dynamic-update-slice_fusion.7
  50.8 0.7 constant_dynamic-update-slice_fusion.5
  52.9 0.7 constant_dynamic-update-slice_fusion.2
  53.6 0.7 constant_dynamic-update-slice_fusion.1
  54.4 0.7 constant_dynamic-update-slice_fusion
  55.1 2.1 copy-done.1
  57.2 6.7 reshape.74
  114.9 6.8 reshape.75
  121.7 7.3 convolution_bitcast_fusion
  129.1 5.8 convolution_bitcast_fusion.1
  135.6 525.4 %all-reduce.6.cloned.1.call-done = f32[2,225,128]{2,1,0:T(8,128)} async-done(((f32[2,225,128]{2,1,0:T(8,128)}), f32[2,225,128]{2,1,0:T(8,128)}) %all-reduce.6.cloned.1.call-update) | async-done | bytes 230416 | tf_op jit(solution)/shard_map/psum | solution.py:57
  661.1 1.0 fusion.6
  662.1 31.6 %collective-permute-start.3 = (bf16[2,225,128]{2,1,0:T(8,128)(2,1)S(1)}, bf16[2,225,128]{2,1,0:T(8,128)(2,1)S(1)}, u32[]{:S(2)}, u32[]{:S(2)}) collective-permute-start(bf16[2,225,128]{2,1,0:T(8,128)(2,1)S(1)} %fusion.6), channel_id=1, source_target_pairs={{1,0},{2,1},{3,2},{5,4},{6,5},{7,6},{9,8},{10,9},{11,10},{13,12},{... | collective-permute-start | bytes 345608 | tf_op jit(solution)/shard_map/ppermute | solution.py:20
  693.6 4.2 collective-permute-start.2
  697.9 6.2 convert_reduce_fusion
  704.1 14.0 %reshape_squeeze.8 = bf16[18225,225]{1,0:T(8,128)(2,1)} reshape(bf16[1,225,81,225]{3,2,1,0:T(8,128)(2,1)} %copy.11) | data formatting | bytes 16402500 | tf_op jit(solution)/shard_map/reshape;squeeze | solution.py:65
  726.2 0.7 constant_dynamic-update-slice_fusion.169
  726.9 0.7 constant_dynamic-update-slice_fusion.168
  729.8 0.7 constant_dynamic-update-slice_fusion.164
  731.3 0.8 constant_dynamic-update-slice_fusion.162
  732.0 2.9 copy.13
  734.9 7.3 reshape.76
  793.1 5.3 copy.16
  798.4 7.4 reshape.77
  805.8 8.8 %fusion.3 = f32[1,225,128]{2,1,0:T(8,128)S(1)} fusion(bf16[18225,128]{1,0:T(8,128)(2,1)} %reshape.76, bf16[18225,225]{1,0:T(8,128)(2,1)} %reshape_squeeze.8, f32[2,1,225,128]{3,2,1,0:T(8,128)S(1)} %copy.9, f32[225]{0:T(256)S(1)} %convert_reduce_fusion), kind=kOutput, calls=%fused_computation.8 | convolution fusion | flops 1049817600 | bytes 13098150 | tf_op jit(solution)/shard_map/dot_general | solution.py:69
  814.6 7.3 fusion.5
  821.9 0.9 copy.17
  (331 shorter events, 123.1 us)
Async XLA Ops:
  6.5 654.5 %all-reduce.6.cloned.1.call-start = ((), (), s32[]{:S(2)}) async-start(), calls=%async_computation | async-start | bytes 475136 | tf_op jit(solution)/shard_map/psum | solution.py:57
  7.5 33.8 %collective-permute-start.1 = (bf16[2,1,225,128]{3,2,1,0:T(8,128)(2,1)S(1)}, bf16[2,1,225,128]{3,2,1,0:T(8,128)(2,1)S(1)}, u32[]{:S(2)}, u32[]{:S(2)}) collective-permute-start(bf16[2,1,225,128]{3,2,1,0:T(8,128)(2,1)S(1)} %copy.22), channel_id=1, source_target_pairs={{1,0},{2,1},{3,2},{5,4},{6,5},{7,6},{9,8},{10,9},{11,10},{13,12},{... | collective-permute-start | bytes 345608 | tf_op jit(solution)/shard_map/ppermute | solution.py:20
  12.6 28.6 %collective-permute-start = (bf16[2,1,225,128]{3,2,1,0:T(8,128)(2,1)S(1)}, bf16[2,1,225,128]{3,2,1,0:T(8,128)(2,1)S(1)}, u32[]{:S(2)}, u32[]{:S(2)}) collective-permute-start(bf16[2,1,225,128]{3,2,1,0:T(8,128)(2,1)S(1)} %copy.22), channel_id=1, source_target_pairs={{0,1},{1,2},{2,3},{4,5},{5,6},{6,7},{8,9},{9,10},{10,11},{12,13},{... | collective-permute-start | bytes 345608 | tf_op jit(solution)/shard_map/ppermute | solution.py:18
  55.1 2.1 copy-start.1
  114.9 14.2 %slice-start = ((s8[4667392]{0:T(1024)(128)(4,1)}), s8[473088]{0:T(1024)(128)(4,1)S(1)}, s32[]{:S(2)}) async-start(s8[4667392]{0:T(1024)(128)(4,1)} %bitcast.1350), calls=%async_computation.1 | async-start | bytes 946176
  121.7 7.3 slice-start.1
  129.1 532.0 %copy-start.3 = (f32[2,225,128]{2,0,1:T(2,128)S(1)}, f32[2,225,128]{2,0,1:T(2,128)}, u32[]{:S(2)}) copy-start(f32[2,225,128]{2,0,1:T(2,128)} %param.5) | copy-start | bytes 691204
  662.1 42.1 %copy-start.2 = (f32[2,1,225,128]{3,1,2,0:T(1,128)S(1)}, f32[2,1,225,128]{3,1,2,0:T(1,128)}, u32[]{:S(2)}) copy-start(f32[2,1,225,128]{3,1,2,0:T(1,128)} %param.3) | copy-start | bytes 691204
  662.1 56.1 %collective-permute-start.3 = (bf16[2,225,128]{2,1,0:T(8,128)(2,1)S(1)}, bf16[2,225,128]{2,1,0:T(8,128)(2,1)S(1)}, u32[]{:S(2)}, u32[]{:S(2)}) collective-permute-start(bf16[2,225,128]{2,1,0:T(8,128)(2,1)S(1)} %fusion.6), channel_id=1, source_target_pairs={{1,0},{2,1},{3,2},{5,4},{6,5},{7,6},{9,8},{10,9},{11,10},{13,12},{... | collective-permute-start | bytes 345608 | tf_op jit(solution)/shard_map/ppermute | solution.py:20
  693.6 24.5 %collective-permute-start.2 = (bf16[2,225,128]{2,1,0:T(8,128)(2,1)S(1)}, bf16[2,225,128]{2,1,0:T(8,128)(2,1)S(1)}, u32[]{:S(2)}, u32[]{:S(2)}) collective-permute-start(bf16[2,225,128]{2,1,0:T(8,128)(2,1)S(1)} %fusion.6), channel_id=1, source_target_pairs={{0,1},{1,2},{2,3},{4,5},{5,6},{6,7},{8,9},{9,10},{10,11},{12,13},{... | collective-permute-start | bytes 345608 | tf_op jit(solution)/shard_map/ppermute | solution.py:18
  805.8 8.8 %copy-start = (bf16[18225,128]{1,0:T(8,128)(2,1)S(1)}, bf16[18225,128]{1,0:T(8,128)(2,1)}, u32[]{:S(2)}) copy-start(bf16[18225,128]{1,0:T(8,128)(2,1)} %reshape.77) | copy-start | bytes 13996804
Sparse Core Ops, SparseCore 0:
  135.8 525.2 all-reduce.5
where the time goes:
time: 831 us; the launch traced here: 830 us
  waiting for transfers between devices  525 us (63%)
  other arithmetic  137 us (16%)
  local copies, waits for them, and re-layouts  80.1 us (10%)
  starting transfers between devices  43.9 us (5%)
  matrix products  29.3 us (4%)
  between operations  14.2 us (2%)
    psum x1, waiting for transfers between devices, local(): projection = lax.psum(partial_value, 'depth')  525 us
    unnamed x303, other arithmetic  126 us
    ppermute x2, starting transfers between devices, with_halo(): lax.ppermute(head, axis, [((i + 1) % count, i) for i in range(ends)])  36.7 us
  transfers between devices with their start and end apart: 5, of which 1 were waited for; matrix products, arithmetic and copies ran while one was open for 6% of the time, Pallas kernels for 0%

commit v1 on v0

--- a/solution.py
+++ b/solution.py
@@ -54,7 +54,8 @@
         total = jnp.dot(flat, spread, preferred_element_type=jnp.float32)
         partial_value.append(total)
     partial_value = jnp.stack(partial_value)
-    projection = lax.psum(partial_value, "depth")
+    blocks = lax.all_gather(partial_value, "depth")
+    projection = jnp.sum(blocks, axis=0)
     ratio = (measured / projection).astype(jnp.bfloat16)
     ratio_rimmed = with_halo(ratio, (("tile", 2),), half * cols)
     spreads = [

time: 831 us -> 617 us (0.74)
  waiting for transfers between devices: 525 us -> 285 us
  starting transfers between devices: 43.9 us -> 56 us
    psum x1 -> x0, waiting for transfers between devices: 525 us -> none  [local(): projection = lax.psum(partial_value, 'depth')]
    all_gather x0 -> x1, waiting for transfers between devices: none -> 285 us  [local(): blocks = lax.all_gather(partial_value, 'depth')]
    ppermute x2, starting transfers between devices: 36.7 us -> 50.1 us  [with_halo(): lax.ppermute(head, axis, [((i + 1) % count, i) for i in range(ends)])]
  transfers between devices with their start and end apart: 5 -> 5, of which waited for: 1 -> 1; matrix products, arithmetic and copies ran while one was open for 6% -> 8% of each run, Pallas kernels for 0% -> 0%
where the time goes in v1:
time: 617 us; the launch traced here: 607 us
  waiting for transfers between devices  285 us (46%)
  other arithmetic  142 us (23%)
  local copies, waits for them, and re-layouts  80.7 us (13%)
  starting transfers between devices  56 us (9%)
  matrix products  29.2 us (5%)
  between operations  14.4 us (2%)
    all_gather x1, waiting for transfers between devices, local(): blocks = lax.all_gather(partial_value, 'depth')  285 us
    unnamed x303, other arithmetic  126 us
    ppermute x2, starting transfers between devices, with_halo(): lax.ppermute(head, axis, [((i + 1) % count, i) for i in range(ends)])  50.1 us
    dot_general x2, matrix products, local(): lax.dot_general(flat, spreads[frame], (((0,), (0,)), ((), ())), preferred...  16.1 us
    another operation x1, local copies, waits for them, and re-layouts, local(): flat = kernel[plane].reshape(phases, offsets * phases)  15.9 us
    reshape x2, local copies, waits for them, and re-layouts, local(): stacked(ratio_rimmed[frame], -1, 1, cols, cells)  14.8 us
    another operation x1, local copies, waits for them, and re-layouts, local(): flat = kernel[plane].reshape(phases * offsets, phases)  14.2 us
    reshape x2, local copies, waits for them, and re-layouts, local(): stacked(rimmed[frame, plane], 1, 0, cols, cells)  13.8 us
  transfers between devices with their start and end apart: 5, of which 1 were waited for; matrix products, arithmetic and copies ran while one was open for 8% of the time, Pallas kernels for 0%

profile of v1, /device:TPU:1, one launch (start us, length us, event | category | flops | bytes accessed | tf_op | source)
XLA Modules:
  0.0 607.5 jit_solution(7642532097806532976)
XLA Ops:
  6.5 1.0 copy.31
  7.5 5.1 collective-permute-start.1
  12.6 3.0 collective-permute-start
  15.7 9.6 %copy.20 = bf16[1,225,81,225]{3,2,1,0:T(8,128)(2,1)} copy(bf16[1,225,81,225]{3,1,2,0:T(8,128)(2,1)} %param.4) | data formatting | bytes 16402500 | tf_op args[1]
  25.4 15.9 %reshape_squeeze.7 = bf16[225,18225]{1,0:T(8,128)(2,1)} reshape(bf16[1,225,81,225]{3,2,1,0:T(8,128)(2,1)} %copy.20) | data formatting | bytes 16402500 | tf_op jit(solution)/shard_map/reshape;squeeze | solution.py:52
  50.8 0.7 constant_dynamic-update-slice_fusion.5
  52.9 0.7 constant_dynamic-update-slice_fusion.2
  53.6 0.7 constant_dynamic-update-slice_fusion.1
  54.4 0.7 constant_dynamic-update-slice_fusion
  55.1 2.1 copy-done.1
  57.2 6.7 %reshape.74 = bf16[18225,128]{1,0:T(8,128)(2,1)} reshape(bf16[81,225,128]{2,1,0:T(8,128)(2,1)} %copy-done.1) | data formatting | bytes 9331200 | tf_op jit(solution)/shard_map/reshape | solution.py:53
  114.9 7.0 %reshape.75 = bf16[18225,128]{1,0:T(8,128)(2,1)} reshape(bf16[81,225,128]{2,1,0:T(8,128)(2,1)} %constant_dynamic-update-slice_fusion.81) | data formatting | bytes 9331200 | tf_op jit(solution)/shard_map/reshape | solution.py:53
  122.0 7.3 %convolution_bitcast_fusion = f32[1,225,128]{2,1,0:T(8,128)S(1)} fusion(bf16[18225,128]{1,0:T(8,128)(2,1)} %reshape.75, bf16[225,18225]{1,0:T(8,128)(2,1)} %reshape_squeeze.7), kind=kOutput, calls=%fused_computation.1 | convolution fusion | flops 1049760000 | bytes 12982050 | tf_op jit(solution)/shard_map/dot_general | solution.py:54
  129.3 5.8 convolution_bitcast_fusion.1
  135.1 0.7 pad_maximum_fusion.2
  135.9 285.1 %all-gather.3.cloned.1.call-done = f32[128,225,128]{2,1,0:T(8,128)} async-done(((f32[2,225,128]{2,1,0:T(8,128)}), f32[128,225,128]{2,1,0:T(8,128)}) %all-gather.3.cloned.1.call-update) | async-done | bytes 14745616 | tf_op jit(solution)/shard_map/all_gather | solution.py:57
  421.0 6.1 %reduce_sum.18 = f32[2,225,128]{2,1,0:T(8,128)S(1)} reduce(f32[64,2,225,128]{3,2,1,0:T(8,128)} %bitcast.1353, f32[]{:T(128)} %constant.48.clone.1), dimensions={0}, to_apply=%region_0.1 | reduce | flops 3628800 | bytes 14976004 | tf_op jit(solution)/shard_map/reduce_sum | solution.py:58
  427.2 44.9 %collective-permute-start.3 = (bf16[2,225,128]{2,1,0:T(8,128)(2,1)S(1)}, bf16[2,225,128]{2,1,0:T(8,128)(2,1)S(1)}, u32[]{:S(2)}, u32[]{:S(2)}) collective-permute-start(bf16[2,225,128]{2,1,0:T(8,128)(2,1)S(1)} %fusion.6), channel_id=1, source_target_pairs={{1,0},{2,1},{3,2},{5,4},{6,5},{7,6},{9,8},{10,9},{11,10},{13,12},{... | collective-permute-start | bytes 345608 | tf_op jit(solution)/shard_map/ppermute | solution.py:20
  472.1 2.9 collective-permute-start.2
  475.1 6.2 %convert_reduce_fusion = f32[225]{0:T(256)S(1)} fusion(bf16[1,225,81,225]{3,1,2,0:T(8,128)(2,1)} %param.4), kind=kLoop, calls=%fused_computation | loop fusion | flops 8201025 | bytes 8202150 | tf_op jit(solution)/shard_map/reduce_sum | solution.py:67
  481.3 14.2 %reshape_squeeze.8 = bf16[18225,225]{1,0:T(8,128)(2,1)} reshape(bf16[1,225,81,225]{3,2,1,0:T(8,128)(2,1)} %copy.20) | data formatting | bytes 16402500 | tf_op jit(solution)/shard_map/reshape;squeeze | solution.py:66
  503.6 0.7 constant_dynamic-update-slice_fusion.169
  504.3 0.7 constant_dynamic-update-slice_fusion.168
  507.2 0.7 constant_dynamic-update-slice_fusion.164
  508.7 0.8 constant_dynamic-update-slice_fusion.162
  509.4 2.9 copy.22
  512.3 7.3 %reshape.76 = bf16[18225,128]{1,0:T(8,128)(2,1)} reshape(bf16[225,81,128]{2,1,0:T(8,128)(2,1)} %copy.22) | data formatting | bytes 9331200 | tf_op jit(solution)/shard_map/reshape | solution.py:62
  570.5 5.3 copy.25
  575.8 7.5 %reshape.77 = bf16[18225,128]{1,0:T(8,128)(2,1)} reshape(bf16[225,81,128]{2,1,0:T(8,128)(2,1)} %copy.25) | data formatting | bytes 9331200 | tf_op jit(solution)/shard_map/reshape | solution.py:62
  583.3 8.8 %fusion.3 = f32[1,225,128]{2,1,0:T(8,128)S(1)} fusion(bf16[18225,128]{1,0:T(8,128)(2,1)} %reshape.76, bf16[18225,225]{1,0:T(8,128)(2,1)} %reshape_squeeze.8, f32[2,1,225,128]{3,2,1,0:T(8,128)S(1)} %copy.18, f32[225]{0:T(256)S(1)} %convert_reduce_fusion), kind=kOutput, calls=%fused_computation.8 | convolution fusion | flops 1049817600 | bytes 13098150 | tf_op jit(solution)/shard_map/dot_general | solution.py:70
  592.2 7.3 %fusion.5 = f32[1,225,128]{2,1,0:T(8,128)S(1)} fusion(bf16[18225,128]{1,0:T(8,128)(2,1)S(1)} %copy-done, bf16[18225,225]{1,0:T(8,128)(2,1)} %reshape_squeeze.8, f32[2,1,225,128]{3,2,1,0:T(8,128)S(1)} %copy.18, f32[225]{0:T(256)S(1)} %convert_reduce_fusion), kind=kOutput, calls=%fused_computation.10 | convolution fusion | flops 1049817600 | bytes 13098150 | tf_op jit(solution)/shard_map/dot_general | solution.py:70
  599.5 0.9 copy.26
  (332 shorter events, 123.2 us)
Async XLA Ops:
  6.5 414.5 %all-gather.3.cloned.1.call-start = ((), (), s32[]{:S(2)}) async-start(), calls=%async_computation | async-start | bytes 15441920 | tf_op jit(solution)/shard_map/all_gather | solution.py:57
  7.5 33.8 %collective-permute-start.1 = (bf16[2,1,225,128]{3,2,1,0:T(8,128)(2,1)S(1)}, bf16[2,1,225,128]{3,2,1,0:T(8,128)(2,1)S(1)}, u32[]{:S(2)}, u32[]{:S(2)}) collective-permute-start(bf16[2,1,225,128]{3,2,1,0:T(8,128)(2,1)S(1)} %copy.31), channel_id=1, source_target_pairs={{1,0},{2,1},{3,2},{5,4},{6,5},{7,6},{9,8},{10,9},{11,10},{13,12},{... | collective-permute-start | bytes 345608 | tf_op jit(solution)/shard_map/ppermute | solution.py:20
  12.6 28.6 %collective-permute-start = (bf16[2,1,225,128]{3,2,1,0:T(8,128)(2,1)S(1)}, bf16[2,1,225,128]{3,2,1,0:T(8,128)(2,1)S(1)}, u32[]{:S(2)}, u32[]{:S(2)}) collective-permute-start(bf16[2,1,225,128]{3,2,1,0:T(8,128)(2,1)S(1)} %copy.31), channel_id=1, source_target_pairs={{0,1},{1,2},{2,3},{4,5},{5,6},{6,7},{8,9},{9,10},{10,11},{12,13},{... | collective-permute-start | bytes 345608 | tf_op jit(solution)/shard_map/ppermute | solution.py:18
  55.1 2.1 copy-start.1
  114.9 14.4 %slice-start = ((s8[4667392]{0:T(1024)(128)(4,1)}), s8[473088]{0:T(1024)(128)(4,1)S(1)}, s32[]{:S(2)}) async-start(s8[4667392]{0:T(1024)(128)(4,1)} %bitcast.1351), calls=%async_computation.1 | async-start | bytes 946176
  121.9 7.4 %slice-start.1 = ((s8[4667392]{0:T(1024)(128)(4,1)}), s8[4194304]{0:T(1024)(128)(4,1)S(1)}, s32[]{:S(2)}) async-start(s8[4667392]{0:T(1024)(128)(4,1)} %bitcast.1351), calls=%async_computation.2 | async-start | bytes 8388608
  421.0 6.1 %copy-start.3 = (f32[2,225,128]{2,0,1:T(2,128)S(1)}, f32[2,225,128]{2,0,1:T(2,128)}, u32[]{:S(2)}) copy-start(f32[2,225,128]{2,0,1:T(2,128)} %param.5) | copy-start | bytes 691204
  427.1 54.2 %copy-start.2 = (f32[2,1,225,128]{3,1,2,0:T(1,128)S(1)}, f32[2,1,225,128]{3,1,2,0:T(1,128)}, u32[]{:S(2)}) copy-start(f32[2,1,225,128]{3,1,2,0:T(1,128)} %param.3) | copy-start | bytes 691204
  427.2 68.4 %collective-permute-start.3 = (bf16[2,225,128]{2,1,0:T(8,128)(2,1)S(1)}, bf16[2,225,128]{2,1,0:T(8,128)(2,1)S(1)}, u32[]{:S(2)}, u32[]{:S(2)}) collective-permute-start(bf16[2,225,128]{2,1,0:T(8,128)(2,1)S(1)} %fusion.6), channel_id=1, source_target_pairs={{1,0},{2,1},{3,2},{5,4},{6,5},{7,6},{9,8},{10,9},{11,10},{13,12},{... | collective-permute-start | bytes 345608 | tf_op jit(solution)/shard_map/ppermute | solution.py:20
  472.1 23.5 %collective-permute-start.2 = (bf16[2,225,128]{2,1,0:T(8,128)(2,1)S(1)}, bf16[2,225,128]{2,1,0:T(8,128)(2,1)S(1)}, u32[]{:S(2)}, u32[]{:S(2)}) collective-permute-start(bf16[2,225,128]{2,1,0:T(8,128)(2,1)S(1)} %fusion.6), channel_id=1, source_target_pairs={{0,1},{1,2},{2,3},{4,5},{5,6},{6,7},{8,9},{9,10},{10,11},{12,13},{... | collective-permute-start | bytes 345608 | tf_op jit(solution)/shard_map/ppermute | solution.py:18
  583.3 8.8 %copy-start = (bf16[18225,128]{1,0:T(8,128)(2,1)S(1)}, bf16[18225,128]{1,0:T(8,128)(2,1)}, u32[]{:S(2)}) copy-start(bf16[18225,128]{1,0:T(8,128)(2,1)} %reshape.77) | copy-start | bytes 13996804
Sparse Core Ops, SparseCore 0:
  136.0 284.9 all-gather.2
